TPU v7x, 128 devices: a whole 4x4x4 slice. The times are simulated.
128 devices in a mesh: row: 8 (over y, x_hi), col: 16 (over x_lo, z, core).
Axes of the slice: x: 4 (x_hi: 2, x_lo: 2; x = x_hi * 2 + x_lo), y: 4, z: 4, core: 2. Of those that a mesh axis runs over, the one named last changes fastest.
Arguments:
- affinity: bfloat16 [8, 16, 32, 256, 256], P('row', 'col'), may hold values from 9e-05 to 32.4
- block_rows: int32 [8, 16, 32], P('row', 'col'), may hold values from 0 to 7, as said below
- block_cols: int32 [8, 16, 32], P('row', 'col'), may hold values from 0 to 15
- block_count: int32 [8, 16], P('row', 'col'), may hold values from 8 to 32, as said below
- labels: float32 [32768, 1024], P(('row', 'col')), may hold values from 0 to 1
- labelled: int32 [32768], P(('row', 'col')), may hold values 0 or 1
Outputs:
- scores: float32 [32768, 1024], P(('row', 'col'))
Inputs may be any that keep to these rules, and one draw needn't show every extreme that they name: Within one entry (r, c) the pairs (block_rows, block_cols) of all 32 slots are distinct, and its first 8 slots name every row block once. `block_count`: some entry has all 32 slots live.
All inputs are finite; a program needn't handle non-finite values. No bound on the sum of `labelled` on one device may be relied on, other than what follows from the above.
Results may differ from a plain program's by a relative error of at most 0.0003.
Values may be sent and summed in bfloat16 or wider, within the bound.
A program may use at most 128 MiB of HBM per device.

v0:
```python
import jax
import jax.numpy as jnp
from jax import lax
from jax.sharding import PartitionSpec as P

SWEEPS = 2
spread_weight = 0.8


def group_term(tile_stack, row_ids, col_ids, slot_live, gathered, group_id, group_width):
    first_slot = group_id * group_width
    tile_group = lax.dynamic_slice_in_dim(tile_stack, first_slot, group_width, 0)
    group_rows = lax.dynamic_slice_in_dim(row_ids, first_slot, group_width, 0)
    group_cols = lax.dynamic_slice_in_dim(col_ids, first_slot, group_width, 0)
    group_live = lax.dynamic_slice_in_dim(slot_live, first_slot, group_width, 0)
    fetched = jnp.take(gathered, group_cols, axis=0)
    product = jnp.einsum("gij,gjc->gic", tile_group, fetched, preferred_element_type=jnp.float32)
    placing = (
        (group_rows[None, :] == jnp.arange(group_width)[:, None]) & group_live[None, :]
    ).astype(jnp.float32)
    return jnp.einsum("rg,gic->ric", placing, product, precision=lax.Precision.HIGHEST)


def on_device(affinity, block_rows, block_cols, block_count, labels, labelled):
    tile_stack = affinity[0, 0]
    row_ids = block_rows[0, 0]
    col_ids = block_cols[0, 0]
    live_count = block_count[0, 0]
    row_groups = lax.axis_size("row")
    col_groups = lax.axis_size("col")
    slot_total = tile_stack.shape[0]
    tile_rows = tile_stack.shape[1]
    classes = labels.shape[1]
    slot_live = jnp.arange(slot_total) < live_count
    placing = ((row_ids[None, :] == jnp.arange(row_groups)[:, None]) & slot_live[None, :]).astype(
        jnp.float32
    )
    row_sums = jnp.sum(tile_stack, axis=2, dtype=jnp.float32)
    degree_part = jnp.dot(placing, row_sums, precision=lax.Precision.HIGHEST)
    degree = lax.psum_scatter(degree_part, "row", scatter_dimension=0, tiled=True).reshape(
        tile_rows, 1
    )
    keep_rows = labelled[:, None] == 1
    current = labels
    group_total = slot_total // row_groups
    for iteration in range(SWEEPS):
        gathered = lax.all_gather(current.astype(jnp.bfloat16), "col", axis=0, tiled=True)
        gathered = gathered.reshape(col_groups, tile_rows, classes)

        def add_group(group_id, running):
            return running + group_term(
                tile_stack, row_ids, col_ids, slot_live, gathered, group_id, row_groups
            )

        empty = jnp.zeros((row_groups, tile_rows, classes), jnp.float32)
        running = lax.fori_loop(0, group_total, add_group, empty)
        flat_terms = running.reshape(row_groups * tile_rows, classes)
        summed = lax.psum_scatter(flat_terms, "row", scatter_dimension=0, tiled=True)
        spread = spread_weight * summed / degree + (1.0 - spread_weight) * labels
        current = jnp.where(keep_rows, labels, spread)
    return current


def solution(mesh):
    placed = (
        P("row", "col", None, None, None),
        P("row", "col", None),
        P("row", "col", None),
        P("row", "col"),
        P(("row", "col"), None),
        P(("row", "col")),
    )
    return jax.shard_map(
        on_device, mesh=mesh, in_specs=placed, out_specs=P(("row", "col"), None), check_vma=False
    )
```

profile of v0, /device:TPU:1, one launch (start us, length us, event | category | flops | bytes accessed | tf_op | source)
XLA Modules:
  0.0 628.7 jit_solution(13757299641391947367)
XLA Ops:
  9.4 55.5 %all-gather.3.cloned.1.call-done = bf16[4096,1024]{1,0:T(8,128)(2,1)} async-done(((bf16[256,1024]{1,0:T(8,128)(2,1)}), bf16[4096,1024]{1,0:T(8,128)(2,1)}) %all-gather.3.cloned.1.call-update) | async-done | bytes 8388624 | tf_op jit(solution)/shard_map/all_gather | solution.py:47
  64.9 125.6 %while.28 = (s32[]{:T(128)}, f32[8,256,1024]{2,0,1:T(8,128)}, s32[32]{0:T(128)}, pred[32]{0:T(512)(128)(4,1)S(1)}, bf16[32,256,256]{2,1,0:T(8,128)(2,1)}, /*inde...) while((s32[]{:T(128)}, f32[8,256,1024]{2,0,1:T(8,128)}, ...), condition=%wide.region_1.3_spmd.clone, body=%wide.region_0.2_spmd.clone.sunk | while | flops 1281361024 | bytes 47191000 | solution.py:56
  71.8 7.1 %fusion.52 = f32[8,256,1024]{2,1,0:T(8,128)} fusion(bf16[8,256,1024]{2,1,0:T(8,128)(2,1)} %gather_fusion, pred[8]{0:T(512)(128)(4,1)S(1)} %get-tuple-element.420, bf16[32,256,256]{2,1,0:T(8,128)(2,1)} %get-tuple-element.456, s32[]{:T(128)S(6)} %select_n.59), kind=kOutput, calls=%fused_computation.5.clone.1 | convolution fusion | flops 1075838976 | bytes 13631500 | tf_op jit(solution)/shard_map/while/body/eval_jaxpr/gij,gjc->gic/dot_general | solution.py:17
  79.0 15.5 %select_add_fusion.4 = f32[8,256,1024]{2,0,1:T(8,128)} fusion(f32[8,256,1024]{2,0,1:T(8,128)} %get-tuple-element.442, pred[]{:T(512)S(6)} %compare.6, f32[8,256,1024]{2,1,0:T(8,128)} %fusion.52, s32[8]{0:T(128)S(1)} %dynamic_slice.79, pred[8]{0:T(512)(128)(4,1)S(1)} %dynamic_slice.80), kind=kOutput, calls=%fused_computation.4.clone.1 | convolution fusion | flops 205521024 | bytes 25165864 | tf_op jit(solution)/shard_map/while/body/eval_jaxpr/rg,gic->ric/dot_general | solution.py:21
  101.4 7.1 %fusion.52 = f32[8,256,1024]{2,1,0:T(8,128)} fusion(bf16[8,256,1024]{2,1,0:T(8,128)(2,1)} %gather_fusion, pred[8]{0:T(512)(128)(4,1)S(1)} %get-tuple-element.420, bf16[32,256,256]{2,1,0:T(8,128)(2,1)} %get-tuple-element.456, s32[]{:T(128)S(6)} %select_n.59), kind=kOutput, calls=%fused_computation.5.clone.1 | convolution fusion | flops 1075838976 | bytes 13631500 | tf_op jit(solution)/shard_map/while/body/eval_jaxpr/gij,gjc->gic/dot_general | solution.py:17
  108.6 17.9 %select_add_fusion.4 = f32[8,256,1024]{2,0,1:T(8,128)} fusion(f32[8,256,1024]{2,0,1:T(8,128)} %get-tuple-element.442, pred[]{:T(512)S(6)} %compare.6, f32[8,256,1024]{2,1,0:T(8,128)} %fusion.52, s32[8]{0:T(128)S(1)} %dynamic_slice.79, pred[8]{0:T(512)(128)(4,1)S(1)} %dynamic_slice.80), kind=kOutput, calls=%fused_computation.4.clone.1 | convolution fusion | flops 205521024 | bytes 25165864 | tf_op jit(solution)/shard_map/while/body/eval_jaxpr/rg,gic->ric/dot_general | solution.py:21
  140.6 17.9 %select_add_fusion.4 = f32[8,256,1024]{2,0,1:T(8,128)} fusion(f32[8,256,1024]{2,0,1:T(8,128)} %get-tuple-element.442, pred[]{:T(512)S(6)} %compare.6, f32[8,256,1024]{2,1,0:T(8,128)} %fusion.52, s32[8]{0:T(128)S(1)} %dynamic_slice.79, pred[8]{0:T(512)(128)(4,1)S(1)} %dynamic_slice.80), kind=kOutput, calls=%fused_computation.4.clone.1 | convolution fusion | flops 205521024 | bytes 25165864 | tf_op jit(solution)/shard_map/while/body/eval_jaxpr/rg,gic->ric/dot_general | solution.py:21
  165.4 7.1 %fusion.52 = f32[8,256,1024]{2,1,0:T(8,128)} fusion(bf16[8,256,1024]{2,1,0:T(8,128)(2,1)} %gather_fusion, pred[8]{0:T(512)(128)(4,1)S(1)} %get-tuple-element.420, bf16[32,256,256]{2,1,0:T(8,128)(2,1)} %get-tuple-element.456, s32[]{:T(128)S(6)} %select_n.59), kind=kOutput, calls=%fused_computation.5.clone.1 | convolution fusion | flops 1075838976 | bytes 13631500 | tf_op jit(solution)/shard_map/while/body/eval_jaxpr/gij,gjc->gic/dot_general | solution.py:17
  172.6 17.9 %select_add_fusion.4 = f32[8,256,1024]{2,0,1:T(8,128)} fusion(f32[8,256,1024]{2,0,1:T(8,128)} %get-tuple-element.442, pred[]{:T(512)S(6)} %compare.6, f32[8,256,1024]{2,1,0:T(8,128)} %fusion.52, s32[8]{0:T(128)S(1)} %dynamic_slice.79, pred[8]{0:T(512)(128)(4,1)S(1)} %dynamic_slice.80), kind=kOutput, calls=%fused_computation.4.clone.1 | convolution fusion | flops 205521024 | bytes 25165864 | tf_op jit(solution)/shard_map/while/body/eval_jaxpr/rg,gic->ric/dot_general | solution.py:21
  190.5 11.5 %copy.9 = f32[8,256,1024]{2,1,0:T(8,128)} copy(f32[8,256,1024]{2,0,1:T(8,128)} %get-tuple-element.254) | data formatting | bytes 16777216 | tf_op jit(solution)/shard_map/while | solution.py:56
  206.6 21.5 %all-reduce = f32[8,256]{1,0:T(8,128)S(1)} all-reduce(f32[8,256]{1,0:T(8,128)S(1)} %fusion.33), channel_id=3, replica_groups=mesh['row'=8,'col'=16] {'row'}, use_global_device_ids=true, to_apply=%region_4.6.clone | all-reduce | flops 2048 | bytes 16384
  228.8 88.5 %reduce-scatter.3.cloned.1.call-done = f32[256,1024]{1,0:T(8,128)} async-done(((f32[2048,1024]{1,0:T(8,128)}), f32[256,1024]{1,0:T(8,128)}) %reduce-scatter.3.cloned.1.call-update) | async-done | bytes 1048592 | tf_op jit(solution)/shard_map/reduce_scatter | solution.py:58
  319.8 51.2 %all-gather.5.cloned.1.call-done = bf16[4096,1024]{1,0:T(8,128)(2,1)} async-done(((bf16[256,1024]{1,0:T(8,128)(2,1)}), bf16[4096,1024]{1,0:T(8,128)(2,1)}) %all-gather.5.cloned.1.call-update) | async-done | bytes 8388624 | tf_op jit(solution)/shard_map/all_gather | solution.py:47
  371.0 122.9 %while.29 = (s32[]{:T(128)}, f32[8,256,1024]{2,0,1:T(8,128)}, s32[32]{0:T(128)S(1)}, pred[32]{0:T(512)(128)(4,1)S(1)}, bf16[32,256,256]{2,1,0:T(8,128)(2,1)}, /*...) while((s32[]{:T(128)}, f32[8,256,1024]{2,0,1:T(8,128)}, ...), condition=%wide.region_6.8_spmd.clone, body=%wide.region_5.7_spmd.clone.sunk | while | flops 1281361024 | bytes 47190460 | solution.py:56
  377.2 7.1 %fusion.57 = f32[8,256,1024]{2,1,0:T(8,128)} fusion(bf16[8,256,1024]{2,1,0:T(8,128)(2,1)} %gather_fusion.1, pred[8]{0:T(512)(128)(4,1)S(1)} %get-tuple-element.429, bf16[32,256,256]{2,1,0:T(8,128)(2,1)} %get-tuple-element.489, s32[]{:T(128)S(6)} %select_n.61), kind=kOutput, calls=%fused_computation.23.clone.1 | convolution fusion | flops 1075838976 | bytes 13631500 | tf_op jit(solution)/shard_map/while/body/eval_jaxpr/gij,gjc->gic/dot_general | solution.py:17
  384.5 15.4 %select_add_fusion.5 = f32[8,256,1024]{2,0,1:T(8,128)} fusion(f32[8,256,1024]{2,0,1:T(8,128)} %get-tuple-element.475, pred[]{:T(512)S(6)} %compare.7, f32[8,256,1024]{2,1,0:T(8,128)} %fusion.57, s32[8]{0:T(128)S(1)} %dynamic_slice.82, pred[8]{0:T(512)(128)(4,1)S(1)} %dynamic_slice.83), kind=kOutput, calls=%fused_computation.22.clone.1 | convolution fusion | flops 205521024 | bytes 25165864 | tf_op jit(solution)/shard_map/while/body/eval_jaxpr/rg,gic->ric/dot_general | solution.py:21
  406.2 7.1 %fusion.57 = f32[8,256,1024]{2,1,0:T(8,128)} fusion(bf16[8,256,1024]{2,1,0:T(8,128)(2,1)} %gather_fusion.1, pred[8]{0:T(512)(128)(4,1)S(1)} %get-tuple-element.429, bf16[32,256,256]{2,1,0:T(8,128)(2,1)} %get-tuple-element.489, s32[]{:T(128)S(6)} %select_n.61), kind=kOutput, calls=%fused_computation.23.clone.1 | convolution fusion | flops 1075838976 | bytes 13631500 | tf_op jit(solution)/shard_map/while/body/eval_jaxpr/gij,gjc->gic/dot_general | solution.py:17
  413.4 17.8 %select_add_fusion.5 = f32[8,256,1024]{2,0,1:T(8,128)} fusion(f32[8,256,1024]{2,0,1:T(8,128)} %get-tuple-element.475, pred[]{:T(512)S(6)} %compare.7, f32[8,256,1024]{2,1,0:T(8,128)} %fusion.57, s32[8]{0:T(128)S(1)} %dynamic_slice.82, pred[8]{0:T(512)(128)(4,1)S(1)} %dynamic_slice.83), kind=kOutput, calls=%fused_computation.22.clone.1 | convolution fusion | flops 205521024 | bytes 25165864 | tf_op jit(solution)/shard_map/while/body/eval_jaxpr/rg,gic->ric/dot_general | solution.py:21
  437.5 7.1 %fusion.57 = f32[8,256,1024]{2,1,0:T(8,128)} fusion(bf16[8,256,1024]{2,1,0:T(8,128)(2,1)} %gather_fusion.1, pred[8]{0:T(512)(128)(4,1)S(1)} %get-tuple-element.429, bf16[32,256,256]{2,1,0:T(8,128)(2,1)} %get-tuple-element.489, s32[]{:T(128)S(6)} %select_n.61), kind=kOutput, calls=%fused_computation.23.clone.1 | convolution fusion | flops 1075838976 | bytes 13631500 | tf_op jit(solution)/shard_map/while/body/eval_jaxpr/gij,gjc->gic/dot_general | solution.py:17
  444.7 17.8 %select_add_fusion.5 = f32[8,256,1024]{2,0,1:T(8,128)} fusion(f32[8,256,1024]{2,0,1:T(8,128)} %get-tuple-element.475, pred[]{:T(512)S(6)} %compare.7, f32[8,256,1024]{2,1,0:T(8,128)} %fusion.57, s32[8]{0:T(128)S(1)} %dynamic_slice.82, pred[8]{0:T(512)(128)(4,1)S(1)} %dynamic_slice.83), kind=kOutput, calls=%fused_computation.22.clone.1 | convolution fusion | flops 205521024 | bytes 25165864 | tf_op jit(solution)/shard_map/while/body/eval_jaxpr/rg,gic->ric/dot_general | solution.py:21
  468.8 7.1 %fusion.57 = f32[8,256,1024]{2,1,0:T(8,128)} fusion(bf16[8,256,1024]{2,1,0:T(8,128)(2,1)} %gather_fusion.1, pred[8]{0:T(512)(128)(4,1)S(1)} %get-tuple-element.429, bf16[32,256,256]{2,1,0:T(8,128)(2,1)} %get-tuple-element.489, s32[]{:T(128)S(6)} %select_n.61), kind=kOutput, calls=%fused_computation.23.clone.1 | convolution fusion | flops 1075838976 | bytes 13631500 | tf_op jit(solution)/shard_map/while/body/eval_jaxpr/gij,gjc->gic/dot_general | solution.py:17
  476.0 17.8 %select_add_fusion.5 = f32[8,256,1024]{2,0,1:T(8,128)} fusion(f32[8,256,1024]{2,0,1:T(8,128)} %get-tuple-element.475, pred[]{:T(512)S(6)} %compare.7, f32[8,256,1024]{2,1,0:T(8,128)} %fusion.57, s32[8]{0:T(128)S(1)} %dynamic_slice.82, pred[8]{0:T(512)(128)(4,1)S(1)} %dynamic_slice.83), kind=kOutput, calls=%fused_computation.22.clone.1 | convolution fusion | flops 205521024 | bytes 25165864 | tf_op jit(solution)/shard_map/while/body/eval_jaxpr/rg,gic->ric/dot_general | solution.py:21
  493.9 11.5 %copy.10 = f32[8,256,1024]{2,1,0:T(8,128)} copy(f32[8,256,1024]{2,0,1:T(8,128)} %get-tuple-element.255) | data formatting | bytes 16777216 | tf_op jit(solution)/shard_map/while | solution.py:56
  505.4 114.3 %reduce-scatter.5.cloned.1.call-done = f32[256,1024]{1,0:T(8,128)} async-done(((f32[2048,1024]{1,0:T(8,128)}), f32[256,1024]{1,0:T(8,128)}) %reduce-scatter.5.cloned.1.call-update) | async-done | bytes 1048592 | tf_op jit(solution)/shard_map/reduce_scatter | solution.py:58
  (78 shorter events, 73.3 us)
Async XLA Ops:
  6.5 58.4 %all-gather.3.cloned.1.call-start = ((), (), s32[]{:S(2)}) async-start(), calls=%async_computation.2 | async-start | bytes 8912896 | tf_op jit(solution)/shard_map/all_gather | solution.py:47
  8.7 308.7 %reduce-scatter.3.cloned.1.call-start = ((), (), s32[]{:S(2)}) async-start(), calls=%async_computation.3 | async-start | bytes 9437184 | tf_op jit(solution)/shard_map/reduce_scatter | solution.py:58
  71.8 7.1 %copy-start.2 = (s32[32]{0:T(128)S(1)}, s32[32]{0:T(128)}, u32[]{:S(2)}) copy-start(s32[32]{0:T(128)} %get-tuple-element.454) | copy-start | bytes 388 | tf_op jit(solution)/shard_map/while
  101.4 7.1 %copy-start.2 = (s32[32]{0:T(128)S(1)}, s32[32]{0:T(128)}, u32[]{:S(2)}) copy-start(s32[32]{0:T(128)} %get-tuple-element.454) | copy-start | bytes 388 | tf_op jit(solution)/shard_map/while
  133.4 7.1 %copy-start.2 = (s32[32]{0:T(128)S(1)}, s32[32]{0:T(128)}, u32[]{:S(2)}) copy-start(s32[32]{0:T(128)} %get-tuple-element.454) | copy-start | bytes 388 | tf_op jit(solution)/shard_map/while
  165.4 7.1 %copy-start.2 = (s32[32]{0:T(128)S(1)}, s32[32]{0:T(128)}, u32[]{:S(2)}) copy-start(s32[32]{0:T(128)} %get-tuple-element.454) | copy-start | bytes 388 | tf_op jit(solution)/shard_map/while
  201.9 0.7 copy-start.5
  201.9 4.6 copy-start.3
  201.9 26.9 %copy-start.4 = (s32[256]{0:T(256)S(1)}, s32[256]{0:T(256)}, u32[]{:S(2)}) copy-start(s32[256]{0:T(256)} %param.17) | copy-start | bytes 3076
  201.9 115.5 %copy-start = (f32[256,1024]{1,0:T(8,128)S(1)}, f32[256,1024]{1,0:T(8,128)}, u32[]{:S(2)}) copy-start(f32[256,1024]{1,0:T(8,128)} %param.16) | copy-start | bytes 3145732
  201.9 169.1 %copy-start.1 = (s32[32]{0:T(128)S(1)}, s32[32]{0:T(128)}, u32[]{:S(2)}) copy-start(s32[32]{0:T(128)} %get-tuple-element.513) | copy-start | bytes 388
  202.0 169.0 %all-gather.5.cloned.1.call-start = ((), (), s32[]{:S(2)}) async-start(), calls=%async_computation.4 | async-start | bytes 8912896 | tf_op jit(solution)/shard_map/all_gather | solution.py:47
  319.7 299.9 %reduce-scatter.5.cloned.1.call-start = ((), (), s32[]{:S(2)}) async-start(), calls=%async_computation.5 | async-start | bytes 9437184 | tf_op jit(solution)/shard_map/reduce_scatter | solution.py:58
Sparse Core Ops, SparseCore 0:
  9.1 55.7 all-gather.2
  202.1 115.2 reduce-scatter.2
  319.9 51.0 all-gather.4
  505.5 114.0 reduce-scatter.4
where the time goes:
time: 630 us; the launch traced here: 629 us
  waiting for transfers between devices  310 us (49%)
  matrix products  195 us (31%)
  local copies, waits for them, and re-layouts  75.3 us (12%)
  blocking collectives  21.5 us (3%)
  between operations  13.9 us (2%)
  other arithmetic  13.6 us (2%)
    reduce_scatter x2, waiting for transfers between devices, on_device(): lax.psum_scatter(flat_terms, 'row', scatter_dimension=0, tiled=True)  203 us
    dot_general x8, matrix products, group_term(): jnp.einsum('rg,gic->ric', placing, product, precision=lax.Precision.HIGHEST)  138 us
    all_gather x2, waiting for transfers between devices, on_device(): lax.all_gather(current.astype(jnp.bfloat16), 'col', axis=0, tiled=True)  107 us
    dot_general x8, matrix products, group_term(): jnp.einsum('gij,gjc->gic', tile_group, fetched, preferred_element_type=jn...  56.6 us
    gather x8, local copies, waits for them, and re-layouts, group_term(): fetched = jnp.take(gathered, group_cols, axis=0)  49.3 us
    while x2, local copies, waits for them, and re-layouts, on_device(): running = lax.fori_loop(0, group_total, add_group, empty)  22.9 us
    unnamed x1, blocking collectives  21.5 us
  transfers between devices with their start and end apart: 4, of which 4 were waited for; matrix products, arithmetic and copies ran while one was open for 1% of the time, Pallas kernels for 0%

commit v1 on v0

--- a/solution.py
+++ b/solution.py
@@ -44,7 +44,9 @@
     current = labels
     group_total = slot_total // row_groups
     for iteration in range(SWEEPS):
-        gathered = lax.all_gather(current.astype(jnp.bfloat16), "col", axis=0, tiled=True)
+        block = current.astype(jnp.bfloat16)
+        stack = jnp.stack([block] * lax.axis_size("col"))
+        gathered = jnp.concatenate(lax.all_to_all(stack, "col", 0, 0), axis=0)
         gathered = gathered.reshape(col_groups, tile_rows, classes)
 
         def add_group(group_id, running):

time: 630 us -> 805 us (1.28); the launches traced: 629 us -> 796 us
  waiting for transfers between devices: 310 us -> 457 us
  starting transfers between devices: 0.13 us -> 13.7 us
  local copies, waits for them, and re-layouts: 75.3 us -> 84 us
    all_to_all x0 -> x2, waiting for transfers between devices: none -> 242 us  [on_device(): gathered = jnp.concatenate(lax.all_to_all(stack, 'col', 0, 0), axis=0)]
    all_gather x2 -> x0, waiting for transfers between devices: 107 us -> none  [on_device(): lax.all_gather(current.astype(jnp.bfloat16), 'col', axis=0, tiled=True)]
    all_to_all x0 -> x2, starting transfers between devices: none -> 13.6 us  [on_device(): gathered = jnp.concatenate(lax.all_to_all(stack, 'col', 0, 0), axis=0)]
    reduce_scatter x2, waiting for transfers between devices: 203 us -> 215 us  [on_device(): lax.psum_scatter(flat_terms, 'row', scatter_dimension=0, tiled=True)]
    another operation x0 -> x2, local copies, waits for them, and re-layouts: none -> 8.66 us  [on_device(): stack = jnp.stack([block] * lax.axis_size('col'))]
where the time goes in v1:
time: 805 us; the launch traced here: 796 us
  waiting for transfers between devices  457 us (57%)
  matrix products  195 us (24%)
  local copies, waits for them, and re-layouts  84 us (10%)
  blocking collectives  21.3 us (3%)
  between operations  14.4 us (2%)
  starting transfers between devices  13.7 us (2%)
  other arithmetic  9.39 us (1%)
    all_to_all x2, waiting for transfers between devices, on_device(): gathered = jnp.concatenate(lax.all_to_all(stack, 'col', 0, 0), axis=0)  242 us
    reduce_scatter x2, waiting for transfers between devices, on_device(): lax.psum_scatter(flat_terms, 'row', scatter_dimension=0, tiled=True)  215 us
    dot_general x8, matrix products, group_term(): jnp.einsum('rg,gic->ric', placing, product, precision=lax.Precision.HIGHEST)  138 us
    dot_general x8, matrix products, group_term(): jnp.einsum('gij,gjc->gic', tile_group, fetched, preferred_element_type=jn...  56.6 us
    gather x8, local copies, waits for them, and re-layouts, group_term(): fetched = jnp.take(gathered, group_cols, axis=0)  49.3 us
    while x2, local copies, waits for them, and re-layouts, on_device(): running = lax.fori_loop(0, group_total, add_group, empty)  22.9 us
    unnamed x1, blocking collectives  21.3 us
  transfers between devices with their start and end apart: 4, of which 4 were waited for; matrix products, arithmetic and copies ran while one was open for 1% of the time, Pallas kernels for 0%

profile of v1, /device:TPU:1, one launch (start us, length us, event | category | flops | bytes accessed | tf_op | source)
XLA Modules:
  0.0 795.6 jit_solution(12558515908850310680)
XLA Ops:
  12.2 7.9 all-to-all-start
  20.8 121.5 %all-to-all-done = bf16[16,256,1024]{2,1,0:T(8,128)(2,1)} async-done(((bf16[16,256,1024]{2,1,0:T(8,128)(2,1)}), bf16[16,256,1024]{2,1,0:T(8,128)(2,1)}, u32[]{:S(2)}, u32[]{:S(2)}) %all-to-all-start) | async-done | bytes 8388640 | tf_op jit(solution)/shard_map/all_to_all | solution.py:49
  142.3 123.3 %while.28 = (s32[]{:T(128)}, f32[8,256,1024]{2,0,1:T(8,128)}, s32[32]{0:T(128)S(1)}, pred[32]{0:T(512)(128)(4,1)S(1)}, bf16[32,256,256]{2,1,0:T(8,128)(2,1)}, /*...) while((s32[]{:T(128)}, f32[8,256,1024]{2,0,1:T(8,128)}, ...), condition=%wide.region_1.3_spmd.clone, body=%wide.region_0.2_spmd.clone.sunk | while | flops 1281361024 | bytes 47190460 | solution.py:58
  148.6 7.1 fusion.52
  155.8 15.4 %select_add_fusion.4 = f32[8,256,1024]{2,0,1:T(8,128)} fusion(f32[8,256,1024]{2,0,1:T(8,128)} %get-tuple-element.442, pred[]{:T(512)S(6)} %compare.6, f32[8,256,1024]{2,1,0:T(8,128)} %fusion.52, s32[8]{0:T(128)S(1)} %dynamic_slice.79, pred[8]{0:T(512)(128)(4,1)S(1)} %dynamic_slice.80), kind=kOutput, calls=%fused_computation.4.clone.1 | convolution fusion | flops 205521024 | bytes 25165864 | tf_op jit(solution)/shard_map/while/body/eval_jaxpr/rg,gic->ric/dot_general | solution.py:21
  177.5 7.1 fusion.52
  184.7 17.8 %select_add_fusion.4 = f32[8,256,1024]{2,0,1:T(8,128)} fusion(f32[8,256,1024]{2,0,1:T(8,128)} %get-tuple-element.442, pred[]{:T(512)S(6)} %compare.6, f32[8,256,1024]{2,1,0:T(8,128)} %fusion.52, s32[8]{0:T(128)S(1)} %dynamic_slice.79, pred[8]{0:T(512)(128)(4,1)S(1)} %dynamic_slice.80), kind=kOutput, calls=%fused_computation.4.clone.1 | convolution fusion | flops 205521024 | bytes 25165864 | tf_op jit(solution)/shard_map/while/body/eval_jaxpr/rg,gic->ric/dot_general | solution.py:21
  208.8 7.1 fusion.52
  216.0 17.8 %select_add_fusion.4 = f32[8,256,1024]{2,0,1:T(8,128)} fusion(f32[8,256,1024]{2,0,1:T(8,128)} %get-tuple-element.442, pred[]{:T(512)S(6)} %compare.6, f32[8,256,1024]{2,1,0:T(8,128)} %fusion.52, s32[8]{0:T(128)S(1)} %dynamic_slice.79, pred[8]{0:T(512)(128)(4,1)S(1)} %dynamic_slice.80), kind=kOutput, calls=%fused_computation.4.clone.1 | convolution fusion | flops 205521024 | bytes 25165864 | tf_op jit(solution)/shard_map/while/body/eval_jaxpr/rg,gic->ric/dot_general | solution.py:21
  240.1 7.1 fusion.52
  247.3 17.8 %select_add_fusion.4 = f32[8,256,1024]{2,0,1:T(8,128)} fusion(f32[8,256,1024]{2,0,1:T(8,128)} %get-tuple-element.442, pred[]{:T(512)S(6)} %compare.6, f32[8,256,1024]{2,1,0:T(8,128)} %fusion.52, s32[8]{0:T(128)S(1)} %dynamic_slice.79, pred[8]{0:T(512)(128)(4,1)S(1)} %dynamic_slice.80), kind=kOutput, calls=%fused_computation.4.clone.1 | convolution fusion | flops 205521024 | bytes 25165864 | tf_op jit(solution)/shard_map/while/body/eval_jaxpr/rg,gic->ric/dot_general | solution.py:21
  265.6 11.5 %copy.9 = f32[8,256,1024]{2,1,0:T(8,128)} copy(f32[8,256,1024]{2,0,1:T(8,128)} %get-tuple-element.254) | data formatting | bytes 16777216 | tf_op jit(solution)/shard_map/while | solution.py:58
  281.8 21.3 %all-reduce = f32[8,256]{1,0:T(8,128)S(1)} all-reduce(f32[8,256]{1,0:T(8,128)S(1)} %fusion.33), channel_id=3, replica_groups=mesh['row'=8,'col'=16] {'row'}, use_global_device_ids=true, to_apply=%region_4.6.clone | all-reduce | flops 2048 | bytes 16384
  303.8 95.5 %reduce-scatter.3.cloned.1.call-done = f32[256,1024]{1,0:T(8,128)} async-done(((f32[2048,1024]{1,0:T(8,128)}), f32[256,1024]{1,0:T(8,128)}) %reduce-scatter.3.cloned.1.call-update) | async-done | bytes 1048592 | tf_op jit(solution)/shard_map/reduce_scatter | solution.py:60
  411.0 120.8 %all-to-all-done.1 = bf16[16,256,1024]{2,1,0:T(8,128)(2,1)} async-done(((bf16[16,256,1024]{2,1,0:T(8,128)(2,1)}), bf16[16,256,1024]{2,1,0:T(8,128)(2,1)}, u32[]{:S(2)}, u32[]{:S(2)}) %all-to-all-start.1) | async-done | bytes 8388640 | tf_op jit(solution)/shard_map/all_to_all | solution.py:49
  531.8 123.2 %while.29 = (s32[]{:T(128)}, f32[8,256,1024]{2,0,1:T(8,128)}, s32[32]{0:T(128)S(1)}, pred[32]{0:T(512)(128)(4,1)S(1)}, bf16[32,256,256]{2,1,0:T(8,128)(2,1)}, /*...) while((s32[]{:T(128)}, f32[8,256,1024]{2,0,1:T(8,128)}, ...), condition=%wide.region_6.8_spmd.clone, body=%wide.region_5.7_spmd.clone.sunk | while | flops 1281361024 | bytes 47190460 | solution.py:58
  538.2 7.1 fusion.57
  545.4 15.5 %select_add_fusion.5 = f32[8,256,1024]{2,0,1:T(8,128)} fusion(f32[8,256,1024]{2,0,1:T(8,128)} %get-tuple-element.475, pred[]{:T(512)S(6)} %compare.7, f32[8,256,1024]{2,1,0:T(8,128)} %fusion.57, s32[8]{0:T(128)S(1)} %dynamic_slice.82, pred[8]{0:T(512)(128)(4,1)S(1)} %dynamic_slice.83), kind=kOutput, calls=%fused_computation.22.clone.1 | convolution fusion | flops 205521024 | bytes 25165864 | tf_op jit(solution)/shard_map/while/body/eval_jaxpr/rg,gic->ric/dot_general | solution.py:21
  574.3 17.8 %select_add_fusion.5 = f32[8,256,1024]{2,0,1:T(8,128)} fusion(f32[8,256,1024]{2,0,1:T(8,128)} %get-tuple-element.475, pred[]{:T(512)S(6)} %compare.7, f32[8,256,1024]{2,1,0:T(8,128)} %fusion.57, s32[8]{0:T(128)S(1)} %dynamic_slice.82, pred[8]{0:T(512)(128)(4,1)S(1)} %dynamic_slice.83), kind=kOutput, calls=%fused_computation.22.clone.1 | convolution fusion | flops 205521024 | bytes 25165864 | tf_op jit(solution)/shard_map/while/body/eval_jaxpr/rg,gic->ric/dot_general | solution.py:21
  605.7 17.8 %select_add_fusion.5 = f32[8,256,1024]{2,0,1:T(8,128)} fusion(f32[8,256,1024]{2,0,1:T(8,128)} %get-tuple-element.475, pred[]{:T(512)S(6)} %compare.7, f32[8,256,1024]{2,1,0:T(8,128)} %fusion.57, s32[8]{0:T(128)S(1)} %dynamic_slice.82, pred[8]{0:T(512)(128)(4,1)S(1)} %dynamic_slice.83), kind=kOutput, calls=%fused_computation.22.clone.1 | convolution fusion | flops 205521024 | bytes 25165864 | tf_op jit(solution)/shard_map/while/body/eval_jaxpr/rg,gic->ric/dot_general | solution.py:21
  629.8 7.1 fusion.57
  637.0 17.8 %select_add_fusion.5 = f32[8,256,1024]{2,0,1:T(8,128)} fusion(f32[8,256,1024]{2,0,1:T(8,128)} %get-tuple-element.475, pred[]{:T(512)S(6)} %compare.7, f32[8,256,1024]{2,1,0:T(8,128)} %fusion.57, s32[8]{0:T(128)S(1)} %dynamic_slice.82, pred[8]{0:T(512)(128)(4,1)S(1)} %dynamic_slice.83), kind=kOutput, calls=%fused_computation.22.clone.1 | convolution fusion | flops 205521024 | bytes 25165864 | tf_op jit(solution)/shard_map/while/body/eval_jaxpr/rg,gic->ric/dot_general | solution.py:21
  655.0 11.5 %copy.10 = f32[8,256,1024]{2,1,0:T(8,128)} copy(f32[8,256,1024]{2,0,1:T(8,128)} %get-tuple-element.255) | data formatting | bytes 16777216 | tf_op jit(solution)/shard_map/while | solution.py:58
  666.5 119.5 %reduce-scatter.5.cloned.1.call-done = f32[256,1024]{1,0:T(8,128)} async-done(((f32[2048,1024]{1,0:T(8,128)}), f32[256,1024]{1,0:T(8,128)}) %reduce-scatter.5.cloned.1.call-update) | async-done | bytes 1048592 | tf_op jit(solution)/shard_map/reduce_scatter | solution.py:60
  (70 shorter events, 90.5 us)
Async XLA Ops:
  12.2 130.1 %copy-start.1 = (s32[1,1,32]{2,1,0:T(1,128)S(1)}, s32[1,1,32]{2,1,0:T(1,128)}, u32[]{:S(2)}) copy-start(s32[1,1,32]{2,1,0:T(1,128)} %param.14) | copy-start | bytes 388
  12.2 130.1 %copy-start.2 = (s32[1,1,32]{2,1,0:T(1,128)S(1)}, s32[1,1,32]{2,1,0:T(1,128)}, u32[]{:S(2)}) copy-start(s32[1,1,32]{2,1,0:T(1,128)} %param.13) | copy-start | bytes 388
  12.2 130.1 %all-to-all-start = ((bf16[16,256,1024]{2,1,0:T(8,128)(2,1)}), bf16[16,256,1024]{2,1,0:T(8,128)(2,1)}, u32[]{:S(2)}, u32[]{:S(2)}) async-start(bf16[16,256,1024]{2,1,0:T(8,128)(2,1)} %stack.4), calls=%async_computation | async-start | bytes 16777216 | tf_op jit(solution)/shard_map/all_to_all | solution.py:49
  20.1 379.2 %reduce-scatter.3.cloned.1.call-start = ((), (), s32[]{:S(2)}) async-start(), calls=%async_computation.4 | async-start | bytes 9437184 | tf_op jit(solution)/shard_map/reduce_scatter | solution.py:60
  277.1 0.7 copy-start.4
  277.1 26.6 %copy-start.3 = (s32[256]{0:T(256)S(1)}, s32[256]{0:T(256)}, u32[]{:S(2)}) copy-start(s32[256]{0:T(256)} %param.17) | copy-start | bytes 3076
  277.1 122.2 %copy-start = (f32[256,1024]{1,0:T(8,128)S(1)}, f32[256,1024]{1,0:T(8,128)}, u32[]{:S(2)}) copy-start(f32[256,1024]{1,0:T(8,128)} %param.16) | copy-start | bytes 3145732
  405.2 126.6 %all-to-all-start.1 = ((bf16[16,256,1024]{2,1,0:T(8,128)(2,1)}), bf16[16,256,1024]{2,1,0:T(8,128)(2,1)}, u32[]{:S(2)}, u32[]{:S(2)}) async-start(bf16[16,256,1024]{2,1,0:T(8,128)(2,1)} %stack.5), calls=%async_computation.2 | async-start | bytes 16777216 | tf_op jit(solution)/shard_map/all_to_all | solution.py:49
  410.9 375.1 %reduce-scatter.5.cloned.1.call-start = ((), (), s32[]{:S(2)}) async-start(), calls=%async_computation.5 | async-start | bytes 9437184 | tf_op jit(solution)/shard_map/reduce_scatter | solution.py:60
Sparse Core Ops, SparseCore 0:
  277.3 121.9 reduce-scatter.2
  666.6 119.3 reduce-scatter.4
